TPU v7x, 32 devices: a whole 2x2x4 slice. The times are simulated.
32 devices in a mesh: grp: 2 (over y), row: 4 (over z), col: 2 (over core), chan: 2 (over x).
Axes of the slice: x: 2, y: 2, z: 4, core: 2. Of those that a mesh axis runs over, the one named last changes fastest.
Arguments:
- theta: bfloat16 [2048, 16, 1024], P(('grp', 'row'), None, ('col', 'chan')), parts along dimension 0, may hold values from -6 to 6
- left_env: bfloat16 [2048, 12, 1024], P(('grp', 'row')), parts along dimension 0, may hold values from -0.25 to 0.25
- right_env: bfloat16 [2048, 12, 1024], P('grp', None, ('col', 'chan')), parts along dimension 0, may hold values from -0.078125 to 0.078125
- mpo_left: float32 [12, 12, 4, 4], replicated, may hold values from -0.875 to 0.875
- mpo_right: float32 [12, 12, 4, 4], replicated, may hold values from -0.875 to 0.875
Outputs:
- residual: bfloat16 [2048, 16384], P(('grp', 'col', 'chan'), 'row'), parts along dimension 0
- hvp: bfloat16 [2048, 16, 1024], P(('grp', 'row'), None, ('col', 'chan')), parts along dimension 0
There are 2 independent parts, one for each index of `grp`. A program takes and returns all parts, laid end to end along the dimension named above; an argument that names none is the same for every part. Nothing has to cross between parts.
All inputs are finite; a program needn't handle non-finite values.
Results may differ from a plain program's by a relative error of at most 0.025.
Values may be sent and summed in bfloat16 or wider, within the bound.
A program may use at most 128 MiB of HBM per device.

v0:
```python
import jax
import jax.numpy as jnp
from jax import lax
from jax.sharding import PartitionSpec as P


def shards(theta, left_env, right_env, mpo_left, mpo_right):
    left_rows = left_env.shape[0]
    channels = left_env.shape[1]
    phys = mpo_left.shape[2]
    phys_pair = theta.shape[1]
    right_rows = theta.shape[2]
    paired = jnp.einsum("wuxs,uvyt->wstxyv", mpo_left, mpo_right, precision=lax.Precision.HIGHEST)
    mpo_pair = paired.reshape(channels * phys * phys, phys * phys * channels).astype(jnp.bfloat16)
    env_block = left_env
    section_one = jnp.einsum(
        "awk,ksb->awsb",
        env_block,
        lax.all_gather(theta, "row", axis=0, tiled=True),
        preferred_element_type=jnp.float32,
    )
    section_one = section_one.astype(jnp.bfloat16).reshape(
        left_rows, channels * phys_pair, right_rows
    )
    section_three = jnp.einsum(
        "pq,apb->aqb", mpo_pair, section_one, preferred_element_type=jnp.float32
    )
    section_three = section_three.astype(jnp.bfloat16).reshape(
        left_rows, phys_pair, channels, right_rows
    )
    env_block = right_env
    term = jnp.einsum("kvb,asvb->kas", env_block, section_three, preferred_element_type=jnp.float32)
    residual_block = lax.psum_scatter(
        term.reshape(right_rows * lax.axis_size(("col", "chan")), left_rows * phys_pair).astype(
            jnp.bfloat16
        ),
        ("col", "chan"),
        scatter_dimension=0,
        tiled=True,
    )
    env_block = right_env
    back_one = jnp.einsum(
        "kp,kvb->pvb",
        lax.all_gather(residual_block, ("col", "chan"), axis=0, tiled=True),
        env_block,
        preferred_element_type=jnp.float32,
    )
    back_one = back_one.astype(jnp.bfloat16).reshape(left_rows, phys_pair * channels, right_rows)
    back_two = jnp.einsum("pq,aqb->apb", mpo_pair, back_one, preferred_element_type=jnp.float32)
    back_two = back_two.astype(jnp.bfloat16).reshape(left_rows, channels, phys_pair, right_rows)
    env_block = left_env
    product = lax.psum_scatter(
        jnp.einsum("awk,awsb->ksb", env_block, back_two, preferred_element_type=jnp.float32).astype(
            jnp.bfloat16
        ),
        "row",
        scatter_dimension=0,
        tiled=True,
    )
    return (residual_block, product)


def solution(mesh):
    in_specs = (
        P(("grp", "row"), None, ("col", "chan")),
        P(("grp", "row"), None, None),
        P("grp", None, ("col", "chan")),
        P(),
        P(),
    )
    out_specs = (P(("grp", "col", "chan"), "row"), P(("grp", "row"), None, ("col", "chan")))
    return jax.shard_map(shards, mesh=mesh, in_specs=in_specs, out_specs=out_specs, check_vma=False)
```

profile of v0, /device:TPU:0, one launch (start us, length us, event | category | flops | bytes accessed | tf_op | source)
XLA Modules:
  0.0 791.3 jit_solution(15360294067785528244)
XLA Ops:
  7.2 0.0 copy-start
  7.2 0.0 all-gather.3.cloned.1.call-start
  7.2 3.6 copy.16
  10.8 0.0 all-gather.3.cloned.1.call-update
  10.9 0.0 reduce-scatter.3.cloned.1.call-start
  10.9 0.0 copy-done
  10.9 2.7 fusion.21
  13.7 2.3 copy.19
  16.0 0.8 convert_element_type.46
  16.7 146.6 %all-gather.3.cloned.1.call-done = bf16[1024,16,256]{2,0,1:T(8,128)(2,1)} async-done(((bf16[256,16,256]{2,0,1:T(8,128)(2,1)}), bf16[1024,16,256]{2,0,1:T(8,128)(2,1)}) %all-gather.3.cloned.1.call-update) | async-done | bytes 8388624 | tf_op jit(solution)/shard_map/all_gather | solution.py:19
  163.4 33.8 %convolution_convert_fusion.2 = bf16[256,12,16,256]{3,0,2,1:T(8,128)(2,1)} fusion(bf16[1024,16,256]{2,0,1:T(8,128)(2,1)} %all-gather.3.cloned.1.call-done, bf16[256,12,1024]{2,0,1:T(8,128)(2,1)} %param.6), kind=kOutput, calls=%fused_computation.9 | convolution fusion | flops 25782386688 | bytes 39845888 | tf_op jit(solution)/shard_map/awk,ksb->awsb/dot_general | solution.py:16
  197.1 71.4 %convert_bitcast_fusion = bf16[256,192,256]{2,1,0:T(8,128)(2,1)} fusion(bf16[256,192,256]{2,0,1:T(8,128)(2,1)} %bitcast.55, bf16[192,192]{1,0:T(8,128)(2,1)S(1)} %convert_element_type.46), kind=kOutput, calls=%fused_computation.4 | convolution fusion | flops 4844421120 | bytes 50405376 | tf_op jit(solution)/shard_map/pq,apb->aqb/dot_general | solution.py:25
  268.5 23.8 %copy.22 = bf16[256,192,256]{2,0,1:T(8,128)(2,1)} copy(bf16[256,192,256]{2,1,0:T(8,128)(2,1)} %convert_bitcast_fusion) | data formatting | bytes 50331648 | tf_op jit(solution)/shard_map/convert_element_type | solution.py:28
  292.3 32.7 %fusion.13 = bf16[1024,256,16]{0,1,2:T(8,128)(2,1)} fusion(bf16[256,16,12,256]{3,0,2,1:T(8,128)(2,1)} %bitcast.57, bf16[1024,12,256]{2,0,1:T(8,128)(2,1)} %param.7), kind=kOutput, calls=%fused_computation.15 | convolution fusion | flops 25773998080 | bytes 39845888 | tf_op jit(solution)/shard_map/kvb,asvb->kas/dot_general | solution.py:32
  325.0 11.3 %copy.23 = bf16[1024,256,16]{0,2,1:T(8,128)(2,1)} copy(bf16[1024,256,16]{0,1,2:T(8,128)(2,1)} %fusion.13) | data formatting | bytes 16777216 | tf_op jit(solution)/shard_map/convert_element_type | solution.py:34
  336.3 0.0 reduce-scatter.3.cloned.1.call-update
  336.3 0.0 all-gather.5.cloned.1.call-start
  336.4 70.0 %reduce-scatter.3.cloned.1.call-done = bf16[256,4096]{0,1:T(8,128)(2,1)} async-done(((bf16[1024,4096]{0,1:T(8,128)(2,1)}), bf16[256,4096]{0,1:T(8,128)(2,1)}) %reduce-scatter.3.cloned.1.call-update) | async-done | bytes 2097168 | tf_op jit(solution)/shard_map/reduce_scatter | solution.py:33
  406.4 0.0 all-gather.5.cloned.1.call-update
  406.4 0.0 reduce-scatter.5.cloned.1.call-start
  406.4 0.8 reshape.33
  407.2 60.3 %all-gather.5.cloned.1.call-done = bf16[1024,4096]{0,1:T(8,128)(2,1)} async-done(((bf16[256,4096]{0,1:T(8,128)(2,1)}), bf16[1024,4096]{0,1:T(8,128)(2,1)}) %all-gather.5.cloned.1.call-update) | async-done | bytes 8388624 | tf_op jit(solution)/shard_map/all_gather | solution.py:44
  467.5 34.2 %convolution_convert_fusion = bf16[4096,12,256]{2,0,1:T(8,128)(2,1)} fusion(bf16[1024,12,256]{2,0,1:T(8,128)(2,1)} %param.7, bf16[1024,4096]{0,1:T(8,128)(2,1)} %all-gather.5.cloned.1.call-done), kind=kOutput, calls=%fused_computation.7 | convolution fusion | flops 25782386688 | bytes 39845888 | tf_op jit(solution)/shard_map/kp,kvb->pvb/dot_general | solution.py:42
  501.6 26.9 %copy.24 = bf16[4096,12,256]{2,1,0:T(8,128)(2,1)} copy(bf16[4096,12,256]{2,0,1:T(8,128)(2,1)} %convolution_convert_fusion) | data formatting | bytes 50331648 | tf_op jit(solution)/shard_map/convert_element_type | solution.py:48
  528.6 40.2 %reshape.23 = bf16[256,192,256]{2,1,0:T(8,128)(2,1)} reshape(bf16[4096,12,256]{2,1,0:T(8,128)(2,1)} %copy.24) | data formatting | bytes 50331648 | tf_op jit(solution)/shard_map/reshape | solution.py:48
  568.7 22.0 %convolution_convert_fusion.1 = bf16[256,256,192]{1,2,0:T(8,128)(2,1)} fusion(bf16[192,192,1]{1,0,2:T(8,128)(2,1)S(1)} %reshape.33, bf16[256,192,256]{2,1,0:T(8,128)(2,1)} %reshape.23), kind=kOutput, calls=%fused_computation.8 | convolution fusion | flops 4844421120 | bytes 50405376 | tf_op jit(solution)/shard_map/pq,aqb->apb/dot_general | solution.py:49
  590.7 44.5 %fusion.16 = bf16[1024,16,256]{0,2,1:T(8,128)(2,1)} fusion(bf16[256,12,1024]{2,0,1:T(8,128)(2,1)} %param.6, bf16[256,12,16,256]{3,2,1,0:T(8,128)(2,1)} %bitcast.54), kind=kOutput, calls=%fused_computation.16 | convolution fusion | flops 25773998080 | bytes 39845888 | tf_op jit(solution)/shard_map/awk,awsb->ksb/dot_general | solution.py:53
  635.2 0.0 reduce-scatter.5.cloned.1.call-update
  635.2 1.6 copy-done.2
  636.8 2.8 copy.26
  639.6 140.2 %reduce-scatter.5.cloned.1.call-done = bf16[256,16,256]{0,2,1:T(8,128)(2,1)} async-done(((bf16[1024,16,256]{0,2,1:T(8,128)(2,1)}), bf16[256,16,256]{0,2,1:T(8,128)(2,1)}) %reduce-scatter.5.cloned.1.call-update) | async-done | bytes 2097168 | tf_op jit(solution)/shard_map/reduce_scatter | solution.py:52
  779.8 4.5 copy.27
  (3 shorter events, 0.0 us)
Async XLA Ops:
  7.2 3.8 copy-start
  7.2 156.2 %all-gather.3.cloned.1.call-start = ((), (), s32[]{:S(2)}) async-start(), calls=%async_computation.2 | async-start | bytes 10485760 | tf_op jit(solution)/shard_map/all_gather | solution.py:19
  10.9 395.5 %reduce-scatter.3.cloned.1.call-start = ((), (), s32[]{:S(2)}) async-start(), calls=%async_computation.3 | async-start | bytes 10485760 | tf_op jit(solution)/shard_map/reduce_scatter | solution.py:33
  336.3 131.1 %all-gather.5.cloned.1.call-start = ((), (), s32[]{:S(2)}) async-start(), calls=%async_computation.4 | async-start | bytes 10485760 | tf_op jit(solution)/shard_map/all_gather | solution.py:44
  406.4 373.4 %reduce-scatter.5.cloned.1.call-start = ((), (), s32[]{:S(2)}) async-start(), calls=%async_computation.5 | async-start | bytes 10485760 | tf_op jit(solution)/shard_map/reduce_scatter | solution.py:52
  635.2 1.6 copy-start.2
  635.2 149.1 %copy-start.1 = (f32[12,12,4,4]{1,3,2,0:T(4,128)S(1)}, f32[12,12,4,4]{1,3,2,0:T(4,128)}, u32[]{:S(2)}) copy-start(f32[12,12,4,4]{1,3,2,0:T(4,128)} %param.8) | copy-start | bytes 27652
Sparse Core Ops, SparseCore 0:
  11.0 152.3 all-gather.2
  336.4 69.8 reduce-scatter.2
  408.0 59.4 all-gather.4
  635.3 144.4 reduce-scatter.4
where the time goes:
time: 800 us; the launch traced here: 791 us
  waiting for transfers between devices  417 us (52%)
  matrix products  241 us (30%)
  local copies, waits for them, and re-layouts  119 us (15%)
  between operations  14.3 us (2%)
    all_gather x1, waiting for transfers between devices, shards(): lax.all_gather(theta, 'row', axis=0, tiled=True)  147 us
    reduce_scatter x1, waiting for transfers between devices, shards(): lax.psum_scatter(jnp.einsum('awk,awsb->ksb', env_block, back_two, preferr...  140 us
    dot_general x1, matrix products, shards(): jnp.einsum('pq,apb->aqb', mpo_pair, section_one, preferred_element_type=j...  71.4 us
    reduce_scatter x1, waiting for transfers between devices, shards(): lax.psum_scatter(term.reshape(right_rows * lax.axis_size(('col', 'chan'))...  70 us
    all_gather x1, waiting for transfers between devices, shards(): lax.all_gather(residual_block, ('col', 'chan'), axis=0, tiled=True)  60.3 us
    dot_general x1, matrix products, shards(): jnp.einsum('awk,awsb->ksb', env_block, back_two, preferred_element_type=j...  44.5 us
    reshape x1, local copies, waits for them, and re-layouts, shards(): back_one.astype(jnp.bfloat16)  40.2 us
    dot_general x1, matrix products, shards(): jnp.einsum('kp,kvb->pvb', lax.all_gather(residual_block, ('col', 'chan'),...  34.2 us
  transfers between devices with their start and end apart: 4, of which 4 were waited for; matrix products, arithmetic and copies ran while one was open for 1% of the time, Pallas kernels for 0%

commit v1 on v0

v1 whole, which is shorter than its diff:
```python
import functools

import jax
import jax.numpy as jnp
from jax import lax
from jax.experimental import pallas as pl
from jax.experimental.pallas import tpu as pltpu
from jax.sharding import PartitionSpec as P

PAD = 16
LIMIT = 52 * 1024 * 1024


def cost(flops, size):
    return pl.CostEstimate(flops=int(flops), bytes_accessed=int(size), transcendentals=0)


def params():
    return pltpu.CompilerParams(dimension_semantics=("arbitrary",), vmem_limit_bytes=LIMIT)


def dot(lhs, rhs):
    return jnp.dot(lhs, rhs, preferred_element_type=jnp.float32)


def forward_kernel(theta_ref, left_ref, mpo_ref, out_ref, lhs, held):
    blocks, rows, width = theta_ref.shape
    channels = left_ref.shape[0]
    tile, _, pairs, lanes = held.shape
    for r in range(blocks):
        lhs[:, r * width : (r + 1) * width] = theta_ref[r]

    def one(w, carry):
        part = dot(lhs[...], left_ref[w]).astype(jnp.bfloat16)
        held[:, w] = part.reshape(tile, pairs, lanes)
        return carry

    lax.fori_loop(0, channels, one, 0, unroll=2)

    def two(b, carry):
        part = dot(mpo_ref[...], held[b].reshape(channels * pairs, lanes)).astype(jnp.bfloat16)
        out_ref[:, b] = part.reshape(out_ref.shape[0], PAD, lanes)
        return carry

    lax.fori_loop(0, tile, two, 0, unroll=8)


def forward(theta, left, mpo, pairs, tile):
    blocks, rows, width = theta.shape
    channels, depth, lanes = left.shape
    bonds = rows // pairs
    step = tile * pairs
    flops = 2 * rows * depth * channels * lanes + 2 * bonds * mpo.size * lanes
    return pl.pallas_call(
        forward_kernel,
        grid=(bonds // tile,),
        out_shape=jax.ShapeDtypeStruct((pairs, bonds, PAD, lanes), jnp.bfloat16),
        in_specs=[
            pl.BlockSpec((blocks, step, width), lambda i: (0, i, 0)),
            pl.BlockSpec(left.shape, lambda i: (0, 0, 0), pipeline_mode=pl.Buffered(1)),
            pl.BlockSpec(mpo.shape, lambda i: (0, 0), pipeline_mode=pl.Buffered(1)),
        ],
        out_specs=pl.BlockSpec((pairs, tile, PAD, lanes), lambda i: (0, i, 0, 0)),
        scratch_shapes=[
            pltpu.VMEM((step, depth), jnp.bfloat16),
            pltpu.VMEM((tile, channels, pairs, lanes), jnp.bfloat16),
        ],
        compiler_params=params(),
        cost_estimate=cost(flops, 2 * (theta.size + left.size + pairs * bonds * PAD * lanes)),
    )(theta, left, mpo)


def residual_kernel(has_total, right_ref, three_ref, *refs):
    out_ref = refs[-1]
    parts, _, rows, lanes = out_ref.shape
    depth = right_ref.shape[1]
    part = dot(right_ref[...], three_ref[0].reshape(depth, lanes))
    part = part.reshape(parts, rows, lanes)
    if has_total:
        part = part + refs[0][:, 0]
    out_ref[:, 0] = part.astype(out_ref.dtype)


def residual_term(right, three, total, chunk, first, count, parts, dtype):
    pairs, bonds, _, lanes = three.shape
    rows = right.shape[0]
    depth = bonds * PAD
    block = (parts, 1, rows // parts, lanes)
    operands = [right, three]
    specs = [
        pl.BlockSpec((rows, depth), lambda i: (0, chunk), pipeline_mode=pl.Buffered(1)),
        pl.BlockSpec((1, bonds, PAD, lanes), lambda i: (first + i, 0, 0, 0)),
    ]
    if total is not None:
        operands.append(total)
        specs.append(pl.BlockSpec(block, lambda i: (0, first + i, 0, 0)))
    aliases = {2: 0} if total is not None and dtype == jnp.float32 else {}
    return pl.pallas_call(
        functools.partial(residual_kernel, total is not None),
        grid=(count,),
        out_shape=jax.ShapeDtypeStruct((parts, count, rows // parts, lanes), dtype),
        in_specs=specs,
        out_specs=pl.BlockSpec(block, lambda i: (0, i, 0, 0)),
        input_output_aliases=aliases,
        compiler_params=params(),
        cost_estimate=cost(2 * rows * depth * count * lanes, count * lanes * (2 * depth + 8 * rows)),
    )(*operands)


def backward_kernel(groups, right_ref, *refs):
    res_refs = refs[:groups]
    mpo_ref, left_ref, out_ref, held, lhs = refs[groups:]
    tile, _, _, lanes = held.shape
    channels = lhs.shape[1] // lanes
    pairs = lhs.shape[0] // tile
    width = out_ref.shape[2]
    begin = 0
    for res_ref in res_refs:
        parts, count, rows, _ = res_ref.shape

        def five(x, carry, res_ref=res_ref, begin=begin, depth=parts * rows):
            part = dot(right_ref[...], res_ref[:, x].reshape(depth, lanes)).astype(jnp.bfloat16)
            held[:, begin + x] = part.reshape(tile, PAD, lanes)
            return carry

        lax.fori_loop(0, count, five, 0, unroll=2)
        begin += count

    def six(b, carry):
        part = dot(mpo_ref[...], held[b].reshape(begin * PAD, lanes)).astype(jnp.bfloat16)
        where = pl.ds(pl.multiple_of(b * pairs, pairs), pairs)
        for w in range(channels):
            lhs[where, w * lanes : (w + 1) * lanes] = part[w * pairs : (w + 1) * pairs]
        return carry

    lax.fori_loop(0, tile, six, 0, unroll=8)

    for r in range(out_ref.shape[0]):
        out_ref[r] = dot(lhs[...], left_ref[:, r * width : (r + 1) * width]).astype(jnp.bfloat16)


def backward(right, residuals, mpo, left, chunk, bonds, pairs, blocks, tile):
    depth, lanes = residuals[0].shape[0] * residuals[0].shape[2], residuals[0].shape[3]
    channels = left.shape[0] // lanes
    width = left.shape[1] // blocks
    steps = bonds // tile
    counts = sum(res.shape[1] for res in residuals)
    flops = 2 * bonds * (PAD * depth * counts * lanes + mpo.size * lanes + pairs * left.size)
    size = 2 * (depth * counts * lanes + left.size + bonds * PAD * depth + bonds * pairs * left.shape[1])
    whole = [
        pl.BlockSpec(res.shape, lambda i: (0, 0, 0, 0), pipeline_mode=pl.Buffered(1))
        for res in residuals
    ]
    return pl.pallas_call(
        functools.partial(backward_kernel, len(residuals)),
        grid=(steps,),
        out_shape=jax.ShapeDtypeStruct((blocks, bonds * pairs, width), jnp.bfloat16),
        in_specs=[pl.BlockSpec((tile * PAD, depth), lambda i: (chunk * steps + i, 0))]
        + whole
        + [
            pl.BlockSpec(mpo.shape, lambda i: (0, 0), pipeline_mode=pl.Buffered(1)),
            pl.BlockSpec(left.shape, lambda i: (0, 0), pipeline_mode=pl.Buffered(1)),
        ],
        out_specs=pl.BlockSpec((blocks, tile * pairs, width), lambda i: (0, i, 0)),
        scratch_shapes=[
            pltpu.VMEM((tile, counts, PAD, lanes), jnp.bfloat16),
            pltpu.VMEM((tile * pairs, channels * lanes), jnp.bfloat16),
        ],
        compiler_params=params(),
        cost_estimate=cost(flops, size),
    )(right, *residuals, mpo, left)


def mpo_product(mpo_left, mpo_right):
    paired = jnp.einsum("wuxs,uvyt->wstxyv", mpo_left, mpo_right, precision=lax.Precision.HIGHEST)
    channels, phys = mpo_left.shape[0], mpo_left.shape[2]
    return paired.reshape(channels * phys * phys, phys * phys * channels).astype(jnp.bfloat16)


def tiled_shards(theta, left_env, right_env, mpo_left, mpo_right):
    lanes, channels, depth = left_env.shape
    pairs, bonds = theta.shape[1:]
    width = theta.shape[0]
    blocks = lax.axis_size("row")
    cols, chans = lax.axis_size("col"), lax.axis_size("chan")
    parts = cols * chans
    chunks = 4
    size = bonds // chunks
    tile = min(32, size)
    halves = 2
    count = pairs // halves
    rows = right_env.shape[0]

    turned = jnp.transpose(theta, (2, 1, 0)).reshape(chunks, size * pairs, width)
    gathered = [lax.all_gather(turned[c], "row", axis=0) for c in range(chunks)]

    mpo = mpo_product(mpo_left, mpo_right).reshape(channels * pairs, pairs, channels)
    mpo = jnp.pad(mpo, ((0, 0), (0, 0), (0, PAD - channels)))
    mpo_back = mpo.reshape(channels * pairs, pairs * PAD)
    mpo_front = mpo_back.T
    left_front = jnp.transpose(left_env, (1, 2, 0))
    left_back = jnp.transpose(left_env, (1, 0, 2)).reshape(channels * lanes, depth)
    right_back = jnp.transpose(right_env, (2, 1, 0))
    right_back = jnp.pad(right_back, ((0, 0), (0, PAD - channels), (0, 0)))
    right_back = right_back.reshape(bonds * PAD, rows)
    right_front = right_back.T

    total = None
    for c in range(chunks - 1):
        three = forward(gathered[c], left_front, mpo_front, pairs, tile)
        total = residual_term(right_front, three, total, c, 0, pairs, parts, jnp.float32)
    three = forward(gathered[-1], left_front, mpo_front, pairs, tile)
    kept, residuals = [], []
    for h in range(halves):
        term = residual_term(
            right_front, three, total, chunks - 1, h * count, count, parts, jnp.bfloat16
        )
        term = term.reshape(cols, chans, count, rows // parts, lanes)
        term = lax.psum_scatter(term, "col", scatter_dimension=0)
        term = lax.psum_scatter(term, "chan", scatter_dimension=0)
        kept.append(term)
    for h in range(halves):
        full = lax.all_gather(lax.all_gather(kept[h], "chan", axis=0), "col", axis=0)
        residuals.append(full.reshape(parts, count, rows // parts, lanes))

    products = []
    for c in range(chunks):
        part = backward(
            right_back, residuals, mpo_back, left_back, c, size, pairs, blocks, tile
        )
        products.append(lax.psum_scatter(part, "row", scatter_dimension=0))
    product = jnp.concatenate(products, axis=0).reshape(bonds, pairs, width)
    residual = jnp.transpose(jnp.concatenate(kept, axis=0), (1, 2, 0))
    return residual.reshape(rows // parts, lanes * pairs), jnp.transpose(product, (2, 1, 0))


def plain_shards(theta, left_env, right_env, mpo_left, mpo_right):
    left_rows, channels = left_env.shape[:2]
    pairs, right_rows = theta.shape[1:]
    mpo_pair = mpo_product(mpo_left, mpo_right)
    einsum = functools.partial(jnp.einsum, preferred_element_type=jnp.float32)
    one = einsum("awk,ksb->awsb", left_env, lax.all_gather(theta, "row", axis=0, tiled=True))
    one = one.astype(jnp.bfloat16).reshape(left_rows, channels * pairs, right_rows)
    three = einsum("pq,apb->aqb", mpo_pair, one).astype(jnp.bfloat16)
    three = three.reshape(left_rows, pairs, channels, right_rows)
    term = einsum("kvb,asvb->kas", right_env, three).astype(jnp.bfloat16)
    term = term.reshape(right_env.shape[0], left_rows * pairs)
    residual = lax.psum_scatter(term, ("col", "chan"), scatter_dimension=0, tiled=True)
    full = lax.all_gather(residual, ("col", "chan"), axis=0, tiled=True)
    back = einsum("kp,kvb->pvb", full, right_env).astype(jnp.bfloat16)
    back = back.reshape(left_rows, pairs * channels, right_rows)
    back = einsum("pq,aqb->apb", mpo_pair, back).astype(jnp.bfloat16)
    back = back.reshape(left_rows, channels, pairs, right_rows)
    product = einsum("awk,awsb->ksb", left_env, back).astype(jnp.bfloat16)
    return residual, lax.psum_scatter(product, "row", scatter_dimension=0, tiled=True)


def shards(theta, left_env, right_env, mpo_left, mpo_right):
    wide = left_env.shape[0] % 128 == 0 and theta.shape[0] % 128 == 0
    wide = wide and theta.shape[2] % 128 == 0 and theta.shape[1] == PAD
    body = tiled_shards if wide and left_env.shape[1] <= PAD else plain_shards
    return body(theta, left_env, right_env, mpo_left, mpo_right)


def solution(mesh):
    in_specs = (
        P(("grp", "row"), None, ("col", "chan")),
        P(("grp", "row"), None, None),
        P("grp", None, ("col", "chan")),
        P(),
        P(),
    )
    out_specs = (P(("grp", "col", "chan"), "row"), P(("grp", "row"), None, ("col", "chan")))
    return jax.shard_map(shards, mesh=mesh, in_specs=in_specs, out_specs=out_specs, check_vma=False)
```

time: 800 us -> 712 us (0.89)
  Pallas kernels: 0 us -> 273 us
  matrix products: 241 us -> 1.86 us
  waiting for transfers between devices: 417 us -> 325 us
  local copies, waits for them, and re-layouts: 119 us -> 85.5 us
    pallas_call x0 -> x13, Pallas kernels: none -> 273 us  [the longest x4 112 us: backward(): pl.pallas_call(functools.partial(backward_kernel, len(residuals)), grid=(...]
    dot_general x7 -> x1, matrix products: 241 us -> 1.86 us  [mpo_product(): jnp.einsum('wuxs,uvyt->wstxyv', mpo_left, mpo_right, precision=lax.Precis...]
    convert_element_type x6 -> x1, local copies, waits for them, and re-layouts: 65.8 us -> 2.45 us  [mpo_product(): paired.reshape(channels * phys * phys, phys * phys * channels)]
    all_gather x2 -> x8, waiting for transfers between devices: 207 us -> 153 us  [the longest x2 67.8 us: tiled_shards(): lax.all_gather(kept[h], 'chan', axis=0)]
    reduce_scatter x2 -> x8, waiting for transfers between devices: 210 us -> 170 us  [the longest x4 93.5 us: tiled_shards(): products.append(lax.psum_scatter(part, 'row', scatter_dimension=0))]
    reshape x1 -> x4, local copies, waits for them, and re-layouts: 40.2 us -> 19.2 us  [the longest x2 15.7 us: tiled_shards(): term = term.reshape(cols, chans, count, rows // parts, lanes)]
    slice x0 -> x5, local copies, waits for them, and re-layouts: none -> 14.1 us  [tiled_shards(): gathered = [lax.all_gather(turned[c], 'row', axis=0) for c in range(chunks)]]
    transpose x0 -> x1, local copies, waits for them, and re-layouts: none -> 11.6 us  [tiled_shards(): right_front = right_back.T]
  transfers between devices with their start and end apart: 4 -> 16, of which waited for: 4 -> 12; matrix products, arithmetic and copies ran while one was open for 1% -> 10% of each run, Pallas kernels for 0% -> 31%
where the time goes in v1:
time: 712 us; the launch traced here: 703 us
  waiting for transfers between devices  325 us (46%)
  Pallas kernels  273 us (38%)
  local copies, waits for them, and re-layouts  85.5 us (12%)
  between operations  14.5 us (2%)
    pallas_call x4, Pallas kernels, backward(): pl.pallas_call(functools.partial(backward_kernel, len(residuals)), grid=(...  112 us
    reduce_scatter x4, waiting for transfers between devices, tiled_shards(): products.append(lax.psum_scatter(part, 'row', scatter_dimension=0))  93.5 us
    pallas_call x5, Pallas kernels, residual_term(): pl.pallas_call(functools.partial(residual_kernel, total is not None), gri...  91.2 us
    pallas_call x4, Pallas kernels, forward(): pl.pallas_call(forward_kernel, grid=(bonds // tile,), out_shape=jax.Shape...  69.5 us
    all_gather x2, waiting for transfers between devices, tiled_shards(): lax.all_gather(kept[h], 'chan', axis=0)  67.8 us
    reduce_scatter x2, waiting for transfers between devices, tiled_shards(): term = lax.psum_scatter(term, 'chan', scatter_dimension=0)  66.8 us
    all_gather x4, waiting for transfers between devices, tiled_shards(): gathered = [lax.all_gather(turned[c], 'row', axis=0) for c in range(chunks)]  54.1 us
    all_gather x2, waiting for transfers between devices, tiled_shards(): lax.all_gather(lax.all_gather(kept[h], 'chan', axis=0), 'col', axis=0)  31.4 us
  transfers between devices with their start and end apart: 16, of which 12 were waited for; matrix products, arithmetic and copies ran while one was open for 10% of the time, Pallas kernels for 31%

profile of v1, /device:TPU:0, one launch (start us, length us, event | category | flops | bytes accessed | tf_op | source)
XLA Modules:
  0.0 703.0 jit_solution(12186515556921323946)
XLA Ops:
  7.2 4.2 fusion.3
  26.7 8.6 %copy.51 = bf16[256,12,1024]{0,2,1:T(8,128)(2,1)} copy(bf16[256,12,1024]{2,0,1:T(8,128)(2,1)} %param.6) | data formatting | bytes 12582912 | tf_op args[1]
  35.3 11.9 %copy.80 = bf16[256,12,1024]{2,1,0:T(8,128)(2,1)} copy(bf16[256,12,1024]{0,2,1:T(8,128)(2,1)} %bitcast.52) | data formatting | bytes 12582912
  47.3 9.0 %pad.8.clone = bf16[256,16,1024]{2,1,0:T(8,128)(2,1)} pad(bf16[256,12,1024]{2,1,0:T(8,128)(2,1)} %copy.80, bf16[]{:T(256)} %constant.2.clone.1), padding=0_0x0_4x0_0 | pad | bytes 14680066 | tf_op jit(solution)/shard_map/jit(_pad)/pad | solution.py:204
  56.2 11.6 %copy.62.right_ref = bf16[1024,4096]{1,0:T(8,128)(2,1)} copy(bf16[1024,4096]{0,1:T(8,128)(2,1)} %bitcast.42) | data formatting | bytes 16777216 | tf_op jit(solution)/shard_map/transpose | solution.py:206
  67.9 17.5 %shard_map.71.three_ref = bf16[16,64,16,256]{3,2,1,0:T(8,128)(2,1)} custom-call(bf16[4,1024,256]{2,1,0:T(8,128)(2,1)} %all-gather.17.cloned.1.call-done.theta_ref, bf16[12,1024,256]{2,1,0:T(8,128)(2,1)} %bitcast.57, bf16[256,192]{1,0:T(8,128)(2,1)S(1)} %bitcast.37), custom_call_target="tpu_custom_call" | custom-call | flops 8053063680 | bytes 16777216 | tf_op jit(solution)/shard_map/pallas_call | solution.py:54
  85.3 24.6 %all-gather.15.cloned.1.call-done.theta_ref = bf16[4,1024,256]{2,1,0:T(8,128)(2,1)} async-done(((bf16[1,1024,256]{2,1,0:T(8,128)(2,1)}), bf16[4,1024,256]{2,1,0:T(8,128)(2,1)}) %all-gather.15.cloned.1.call-update) | async-done | bytes 2097168 | tf_op jit(solution)/shard_map/all_gather | solution.py:195
  109.9 17.3 %shard_map.70.three_ref = bf16[16,64,16,256]{3,2,1,0:T(8,128)(2,1)} custom-call(bf16[4,1024,256]{2,1,0:T(8,128)(2,1)} %all-gather.15.cloned.1.call-done.theta_ref, bf16[12,1024,256]{2,1,0:T(8,128)(2,1)} %bitcast.58, bf16[256,192]{1,0:T(8,128)(2,1)S(1)} %bitcast.38), custom_call_target="tpu_custom_call" | custom-call | flops 8053063680 | bytes 16777216 | tf_op jit(solution)/shard_map/pallas_call | solution.py:54
  127.3 29.5 %all-gather.13.cloned.1.call-done.theta_ref = bf16[4,1024,256]{2,1,0:T(8,128)(2,1)} async-done(((bf16[1,1024,256]{2,1,0:T(8,128)(2,1)}), bf16[4,1024,256]{2,1,0:T(8,128)(2,1)}) %all-gather.13.cloned.1.call-update) | async-done | bytes 2097168 | tf_op jit(solution)/shard_map/all_gather | solution.py:195
  156.8 17.3 %shard_map.69.three_ref = bf16[16,64,16,256]{3,2,1,0:T(8,128)(2,1)} custom-call(bf16[4,1024,256]{2,1,0:T(8,128)(2,1)} %all-gather.13.cloned.1.call-done.theta_ref, bf16[12,1024,256]{2,1,0:T(8,128)(2,1)} %bitcast.59, bf16[256,192]{1,0:T(8,128)(2,1)S(1)} %bitcast.39), custom_call_target="tpu_custom_call" | custom-call | flops 8053063680 | bytes 16777216 | tf_op jit(solution)/shard_map/pallas_call | solution.py:54
  174.1 19.4 %shard_map.72.refs_0_ = f32[4,16,256,256]{3,2,1,0:T(8,128)} custom-call(bf16[1024,4096]{1,0:T(8,128)(2,1)} %copy.62.right_ref, bf16[16,64,16,256]{3,2,1,0:T(8,128)(2,1)} %shard_map.71.three_ref), custom_call_target="tpu_custom_call" | custom-call | flops 8589934592 | bytes 41943040 | tf_op jit(solution)/shard_map/pallas_call | solution.py:98
  193.6 23.9 %shard_map.73.refs_0_ = f32[4,16,256,256]{3,2,1,0:T(8,128)} custom-call(bf16[1024,4096]{1,0:T(8,128)(2,1)} %copy.62.right_ref, bf16[16,64,16,256]{3,2,1,0:T(8,128)(2,1)} %shard_map.70.three_ref, f32[4,16,256,256]{3,2,1,0:T(8,128)} %shard_map.72.refs_0_), custom_call_target="tpu_custom_call", output_to_operand_aliasing={{}: (2, {})} | custom-call | flops 8589934592 | bytes 41943040 | tf_op jit(solution)/shard_map/pallas_call | solution.py:98
  217.4 23.9 %shard_map.74.refs_0_ = f32[4,16,256,256]{3,2,1,0:T(8,128)} custom-call(bf16[1024,4096]{1,0:T(8,128)(2,1)} %copy.62.right_ref, bf16[16,64,16,256]{3,2,1,0:T(8,128)(2,1)} %shard_map.69.three_ref, f32[4,16,256,256]{3,2,1,0:T(8,128)} %shard_map.73.refs_0_), custom_call_target="tpu_custom_call", output_to_operand_aliasing={{}: (2, {})} | custom-call | flops 8589934592 | bytes 41943040 | tf_op jit(solution)/shard_map/pallas_call | solution.py:98
  241.3 17.4 %shard_map.68.three_ref = bf16[16,64,16,256]{3,2,1,0:T(8,128)(2,1)} custom-call(bf16[4,1024,256]{2,1,0:T(8,128)(2,1)} %all-gather.11.cloned.1.call-done.theta_ref, bf16[12,1024,256]{2,1,0:T(8,128)(2,1)} %bitcast.60, bf16[256,192]{1,0:T(8,128)(2,1)S(1)} %bitcast.40), custom_call_target="tpu_custom_call" | custom-call | flops 8053063680 | bytes 16777216 | tf_op jit(solution)/shard_map/pallas_call | solution.py:54
  258.7 11.6 %shard_map.75 = bf16[4,8,256,256]{3,2,1,0:T(8,128)(2,1)} custom-call(bf16[1024,4096]{1,0:T(8,128)(2,1)} %copy.62.right_ref, bf16[16,64,16,256]{3,2,1,0:T(8,128)(2,1)} %shard_map.68.three_ref, f32[4,16,256,256]{3,2,1,0:T(8,128)} %shard_map.74.refs_0_), custom_call_target="tpu_custom_call" | custom-call | flops 4294967296 | bytes 20971520 | tf_op jit(solution)/shard_map/pallas_call | solution.py:98
  270.3 7.8 %copy.63 = bf16[2,2,8,256,256]{3,2,4,1,0:T(8,128)(2,1)} copy(bf16[2,2,8,256,256]{4,3,2,1,0:T(8,128)(2,1)} %bitcast.48) | data formatting | bytes 8388608 | tf_op jit(solution)/shard_map/reshape | solution.py:218
  278.2 12.4 %shard_map.76 = bf16[4,8,256,256]{3,2,1,0:T(8,128)(2,1)} custom-call(bf16[1024,4096]{1,0:T(8,128)(2,1)} %copy.62.right_ref, bf16[16,64,16,256]{3,2,1,0:T(8,128)(2,1)} %shard_map.68.three_ref, f32[4,16,256,256]{3,2,1,0:T(8,128)} %shard_map.74.refs_0_), custom_call_target="tpu_custom_call" | custom-call | flops 4294967296 | bytes 20971520 | tf_op jit(solution)/shard_map/pallas_call | solution.py:98
  290.7 7.8 %copy.65 = bf16[2,2,8,256,256]{3,2,4,1,0:T(8,128)(2,1)} copy(bf16[2,2,8,256,256]{4,3,2,1,0:T(8,128)(2,1)} %bitcast.47) | data formatting | bytes 8388608 | tf_op jit(solution)/shard_map/reshape | solution.py:218
  299.3 10.1 %reduce-scatter.13.cloned.1.call-done = bf16[1,2,8,256,256]{3,2,4,1,0:T(8,128)(2,1)} async-done(((bf16[2,2,8,256,256]{3,2,4,1,0:T(8,128)(2,1)}), bf16[1,2,8,256,256]{3,2,4,1,0:T(8,128)(2,1)}) %reduce-scatter.13.cloned.1.call-update) | async-done | bytes 2097168 | tf_op jit(solution)/shard_map/reduce_scatter | solution.py:219
  309.5 35.3 %reduce-scatter.11.cloned.1.call-done = bf16[1,8,256,256]{2,1,3,0:T(8,128)(2,1)} async-done(((bf16[2,8,256,256]{2,1,3,0:T(8,128)(2,1)}), bf16[1,8,256,256]{2,1,3,0:T(8,128)(2,1)}) %reduce-scatter.11.cloned.1.call-update) | async-done | bytes 1048592 | tf_op jit(solution)/shard_map/reduce_scatter | solution.py:220
  347.4 31.5 %reduce-scatter.15.cloned.1.call-done = bf16[1,8,256,256]{2,1,3,0:T(8,128)(2,1)} async-done(((bf16[2,8,256,256]{2,1,3,0:T(8,128)(2,1)}), bf16[1,8,256,256]{2,1,3,0:T(8,128)(2,1)}) %reduce-scatter.15.cloned.1.call-update) | async-done | bytes 1048592 | tf_op jit(solution)/shard_map/reduce_scatter | solution.py:220
  381.5 32.8 %all-gather.19.cloned.1.call-done = bf16[2,8,256,256]{3,2,1,0:T(8,128)(2,1)} async-done(((bf16[1,8,256,256]{3,2,1,0:T(8,128)(2,1)}), bf16[2,8,256,256]{3,2,1,0:T(8,128)(2,1)}) %all-gather.19.cloned.1.call-update) | async-done | bytes 2097168 | tf_op jit(solution)/shard_map/all_gather | solution.py:223
  414.3 35.0 %all-gather.21.cloned.1.call-done = bf16[2,8,256,256]{3,2,1,0:T(8,128)(2,1)} async-done(((bf16[1,8,256,256]{3,2,1,0:T(8,128)(2,1)}), bf16[2,8,256,256]{3,2,1,0:T(8,128)(2,1)}) %all-gather.21.cloned.1.call-update) | async-done | bytes 2097168 | tf_op jit(solution)/shard_map/all_gather | solution.py:223
  449.6 15.1 %all-gather.23.cloned.1.call-done.refs_0_ = bf16[4,8,256,256]{3,2,1,0:T(8,128)(2,1)} async-done(((bf16[2,8,256,256]{3,2,1,0:T(8,128)(2,1)}), bf16[4,8,256,256]{3,2,1,0:T(8,128)(2,1)}) %all-gather.23.cloned.1.call-update) | async-done | bytes 4194320 | tf_op jit(solution)/shard_map/all_gather | solution.py:223
  464.6 16.3 %all-gather.25.cloned.1.call-done.refs_1_ = bf16[4,8,256,256]{3,2,1,0:T(8,128)(2,1)} async-done(((bf16[2,8,256,256]{3,2,1,0:T(8,128)(2,1)}), bf16[4,8,256,256]{3,2,1,0:T(8,128)(2,1)}) %all-gather.25.cloned.1.call-update) | async-done | bytes 4194320 | tf_op jit(solution)/shard_map/all_gather | solution.py:223
  480.9 27.9 %shard_map.77 = bf16[4,1024,256]{2,1,0:T(8,128)(2,1)} custom-call(bf16[4096,1024]{1,0:T(8,128)(2,1)} %bitcast.43, bf16[4,8,256,256]{3,2,1,0:T(8,128)(2,1)} %all-gather.23.cloned.1.call-done.refs_0_, bf16[4,8,256,256]{3,2,1,0:T(8,128)(2,1)} %all-gather.25.cloned.1.call-done.refs_1_, bf16[192,256]{1,0:T(8,128)(2,1)S(1)} %copy.68.refs_2_, ...), custom_call_target="tpu_custom_call" | custom-call | flops 16642998272 | bytes 18874368 | tf_op jit(solution)/shard_map/pallas_call | solution.py:154
  508.9 27.9 %shard_map.78 = bf16[4,1024,256]{2,1,0:T(8,128)(2,1)} custom-call(bf16[4096,1024]{1,0:T(8,128)(2,1)} %bitcast.44, bf16[4,8,256,256]{3,2,1,0:T(8,128)(2,1)} %all-gather.23.cloned.1.call-done.refs_0_, bf16[4,8,256,256]{3,2,1,0:T(8,128)(2,1)} %all-gather.25.cloned.1.call-done.refs_1_, bf16[192,256]{1,0:T(8,128)(2,1)S(1)} %copy.68.refs_2_, ...), custom_call_target="tpu_custom_call" | custom-call | flops 16642998272 | bytes 18874368 | tf_op jit(solution)/shard_map/pallas_call | solution.py:154
  536.8 28.0 %shard_map.79 = bf16[4,1024,256]{2,1,0:T(8,128)(2,1)} custom-call(bf16[4096,1024]{1,0:T(8,128)(2,1)} %bitcast.45, bf16[4,8,256,256]{3,2,1,0:T(8,128)(2,1)} %all-gather.23.cloned.1.call-done.refs_0_, bf16[4,8,256,256]{3,2,1,0:T(8,128)(2,1)} %all-gather.25.cloned.1.call-done.refs_1_, bf16[192,256]{1,0:T(8,128)(2,1)S(1)} %copy.68.refs_2_, ...), custom_call_target="tpu_custom_call" | custom-call | flops 16642998272 | bytes 18874368 | tf_op jit(solution)/shard_map/pallas_call | solution.py:154
  564.9 28.2 %shard_map.80 = bf16[4,1024,256]{2,1,0:T(8,128)(2,1)} custom-call(bf16[4096,1024]{1,0:T(8,128)(2,1)} %bitcast.46, bf16[4,8,256,256]{3,2,1,0:T(8,128)(2,1)} %all-gather.23.cloned.1.call-done.refs_0_, bf16[4,8,256,256]{3,2,1,0:T(8,128)(2,1)} %all-gather.25.cloned.1.call-done.refs_1_, bf16[192,256]{1,0:T(8,128)(2,1)S(1)} %copy.68.refs_2_, ...), custom_call_target="tpu_custom_call" | custom-call | flops 16642998272 | bytes 18874368 | tf_op jit(solution)/shard_map/pallas_call | solution.py:154
  599.6 45.3 %reduce-scatter.21.cloned.1.call-done = bf16[1,1024,256]{2,1,0:T(8,128)(2,1)} async-done(((bf16[4,1024,256]{2,1,0:T(8,128)(2,1)}), bf16[1,1024,256]{2,1,0:T(8,128)(2,1)}) %reduce-scatter.21.cloned.1.call-update) | async-done | bytes 524304 | tf_op jit(solution)/shard_map/reduce_scatter | solution.py:231
  644.8 46.0 %reduce-scatter.23.cloned.1.call-done = bf16[1,1024,256]{2,1,0:T(8,128)(2,1)} async-done(((bf16[4,1024,256]{2,1,0:T(8,128)(2,1)}), bf16[1,1024,256]{2,1,0:T(8,128)(2,1)}) %reduce-scatter.23.cloned.1.call-update) | async-done | bytes 524304 | tf_op jit(solution)/shard_map/reduce_scatter | solution.py:231
  692.6 3.5 copy.72
  (59 shorter events, 29.8 us)
Async XLA Ops:
  7.2 14.5 %copy-start = (f32[12,12,4,4]{1,3,2,0:T(4,128)S(1)}, f32[12,12,4,4]{1,3,2,0:T(4,128)}, u32[]{:S(2)}) copy-start(f32[12,12,4,4]{1,3,2,0:T(4,128)} %param.8) | copy-start | bytes 27652
  7.2 60.7 %all-gather.17.cloned.1.call-start = ((), (), s32[]{:S(2)}) async-start(), calls=%async_computation.11 | async-start | bytes 2621440 | tf_op jit(solution)/shard_map/all_gather | solution.py:195
  11.5 10.2 %copy-start.3 = (f32[12,12,4,4]{1,3,2,0:T(4,128)S(1)}, f32[12,12,4,4]{1,3,2,0:T(4,128)}, u32[]{:S(2)}) copy-start(f32[12,12,4,4]{1,3,2,0:T(4,128)} %param.9) | copy-start | bytes 27652
  14.9 95.0 %all-gather.15.cloned.1.call-start = ((), (), s32[]{:S(2)}) async-start(), calls=%async_computation.10 | async-start | bytes 2621440 | tf_op jit(solution)/shard_map/all_gather | solution.py:195
  17.2 139.6 %all-gather.13.cloned.1.call-start = ((), (), s32[]{:S(2)}) async-start(), calls=%async_computation.9 | async-start | bytes 2621440 | tf_op jit(solution)/shard_map/all_gather | solution.py:195
  19.4 221.9 %all-gather.11.cloned.1.call-start = ((), (), s32[]{:S(2)}) async-start(), calls=%async_computation.8 | async-start | bytes 2621440 | tf_op jit(solution)/shard_map/all_gather | solution.py:195
  21.6 277.0 %reduce-scatter.9.cloned.1.call-start = ((), (), s32[]{:S(2)}) async-start(), calls=%async_computation.12 | async-start | bytes 6291456 | tf_op jit(solution)/shard_map/reduce_scatter | solution.py:219
  278.2 31.2 %reduce-scatter.13.cloned.1.call-start = ((), (), s32[]{:S(2)}) async-start(), calls=%async_computation.14 | async-start | bytes 6291456 | tf_op jit(solution)/shard_map/reduce_scatter | solution.py:219
  298.5 46.3 %reduce-scatter.11.cloned.1.call-start = ((), (), s32[]{:S(2)}) async-start(), calls=%async_computation.13 | async-start | bytes 3145728 | tf_op jit(solution)/shard_map/reduce_scatter | solution.py:220
  299.3 79.7 %reduce-scatter.15.cloned.1.call-start = ((), (), s32[]{:S(2)}) async-start(), calls=%async_computation.15 | async-start | bytes 3145728 | tf_op jit(solution)/shard_map/reduce_scatter | solution.py:220
  309.4 104.8 %all-gather.19.cloned.1.call-start = ((), (), s32[]{:S(2)}) async-start(), calls=%async_computation.16 | async-start | bytes 3145728 | tf_op jit(solution)/shard_map/all_gather | solution.py:223
  347.4 102.0 %all-gather.21.cloned.1.call-start = ((), (), s32[]{:S(2)}) async-start(), calls=%async_computation.17 | async-start | bytes 3145728 | tf_op jit(solution)/shard_map/all_gather | solution.py:223
  381.4 83.2 %all-gather.23.cloned.1.call-start = ((), (), s32[]{:S(2)}) async-start(), calls=%async_computation.22 | async-start | bytes 6291456 | tf_op jit(solution)/shard_map/all_gather | solution.py:223
  414.3 66.6 %all-gather.25.cloned.1.call-start = ((), (), s32[]{:S(2)}) async-start(), calls=%async_computation.23 | async-start | bytes 6291456 | tf_op jit(solution)/shard_map/all_gather | solution.py:223
  449.4 148.0 %reduce-scatter.17.cloned.1.call-start = ((), (), s32[]{:S(2)}) async-start(), calls=%async_computation.18 | async-start | bytes 2621440 | tf_op jit(solution)/shard_map/reduce_scatter | solution.py:231
  508.8 90.8 %reduce-scatter.19.cloned.1.call-start = ((), (), s32[]{:S(2)}) async-start(), calls=%async_computation.19 | async-start | bytes 2621440 | tf_op jit(solution)/shard_map/reduce_scatter | solution.py:231
  536.8 108.0 %reduce-scatter.21.cloned.1.call-start = ((), (), s32[]{:S(2)}) async-start(), calls=%async_computation.20 | async-start | bytes 2621440 | tf_op jit(solution)/shard_map/reduce_scatter | solution.py:231
  564.8 28.3 %copy-start.2 = (bf16[1,8,256,256]{2,1,3,0:T(8,128)(2,1)S(1)}, bf16[1,8,256,256]{2,1,3,0:T(8,128)(2,1)}, u32[]{:S(2)}) copy-start(bf16[1,8,256,256]{2,1,3,0:T(8,128)(2,1)} %reduce-scatter.11.cloned.1.call-done) | copy-start | bytes 3145732
  564.9 126.0 %reduce-scatter.23.cloned.1.call-start = ((), (), s32[]{:S(2)}) async-start(), calls=%async_computation.21 | async-start | bytes 2621440 | tf_op jit(solution)/shard_map/reduce_scatter | solution.py:231
  690.9 5.1 copy-start.1
Sparse Core Ops, SparseCore 0:
  15.0 48.6 all-gather.16
  65.3 44.6 all-gather.14
  112.1 44.6 all-gather.12
  158.8 44.6 all-gather.10
  278.3 10.6 reduce-scatter.8
  298.6 10.7 reduce-scatter.12
  311.6 33.0 reduce-scatter.10
  347.1 31.8 reduce-scatter.14
  381.1 33.1 all-gather.18
  416.2 33.1 all-gather.20
  450.9 13.6 all-gather.22
  466.0 14.8 all-gather.24
  508.9 45.0 reduce-scatter.16
  556.3 43.2 reduce-scatter.18
  601.7 43.0 reduce-scatter.20
  647.7 43.1 reduce-scatter.22

commit v2 on v1

v2 whole, which is shorter than its diff:
```python
import functools

import jax
import jax.numpy as jnp
from jax import lax
from jax.experimental import pallas as pl
from jax.experimental.pallas import tpu as pltpu
from jax.sharding import PartitionSpec as P

PAD = 16
LIMIT = 52 * 1024 * 1024


def cost(flops, size):
    return pl.CostEstimate(flops=int(flops), bytes_accessed=int(size), transcendentals=0)


def params():
    return pltpu.CompilerParams(dimension_semantics=("arbitrary",), vmem_limit_bytes=LIMIT)


def dot(lhs, rhs):
    return jnp.dot(lhs, rhs, preferred_element_type=jnp.float32)


def pair_dot(lhs, first, second):
    return dot(lhs, jnp.concatenate([first, second], axis=1)).astype(jnp.bfloat16)


def forward_kernel(tiles, has_total, theta_ref, left_ref, mpo_ref, right_ref, *refs):
    out_ref, lhs, held, three = refs[-4:]
    blocks, _, width = theta_ref.shape
    tile, channels, pairs, lanes = held.shape
    parts, _, rows, _ = out_ref.shape
    depth = right_ref.shape[1]
    index = pl.program_id(0)

    @pl.when(index < tiles)
    def _():
        for r in range(blocks):
            lhs[:, r * width : (r + 1) * width] = theta_ref[r]

        def one(w, carry):
            part = dot(lhs[...], left_ref[w]).astype(jnp.bfloat16)
            held[:, 2 * w] = part[:, :lanes].reshape(tile, pairs, lanes)
            held[:, 2 * w + 1] = part[:, lanes:].reshape(tile, pairs, lanes)
            return carry

        lax.fori_loop(0, channels // 2, one, 0, unroll=2)

        def two(b, carry):
            first = held[2 * b].reshape(channels * pairs, lanes)
            second = held[2 * b + 1].reshape(channels * pairs, lanes)
            part = pair_dot(mpo_ref[...], first, second)
            where = index * tile + 2 * b
            three[:, where] = part[:, :lanes].reshape(three.shape[0], PAD, lanes)
            three[:, where + 1] = part[:, lanes:].reshape(three.shape[0], PAD, lanes)
            return carry

        lax.fori_loop(0, tile // 2, two, 0, unroll=4)

    @pl.when(index >= tiles)
    def _():
        x = 2 * (index - tiles)
        first, second = three[x].reshape(depth, lanes), three[x + 1].reshape(depth, lanes)
        part = dot(right_ref[...], jnp.concatenate([first, second], axis=1))
        for j in range(2):
            term = part[:, j * lanes : (j + 1) * lanes].reshape(parts, rows, lanes)
            if has_total:
                term = term + refs[0][:, j]
            out_ref[:, j] = term.astype(out_ref.dtype)


def forward(theta, left, mpo, right, total, chunk, pairs, tile, parts, dtype):
    blocks, steps, width = theta.shape
    halves, depth, twice = left.shape
    lanes, channels = twice // 2, halves * 2
    bonds = steps // pairs
    tiles = bonds // tile
    rows = right.shape[0]
    step = tile * pairs
    flops = 2 * steps * depth * channels * lanes + 2 * bonds * mpo.size * lanes
    flops += 2 * rows * bonds * PAD * pairs * lanes
    block = (parts, 2, rows // parts, lanes)
    late = lambda i: (0, jnp.maximum(i - tiles, 0), 0, 0)
    operands = [theta, left, mpo, right]
    specs = [
        pl.BlockSpec((blocks, step, width), lambda i: (0, jnp.minimum(i, tiles - 1), 0)),
        pl.BlockSpec(left.shape, lambda i: (0, 0, 0), pipeline_mode=pl.Buffered(1)),
        pl.BlockSpec(mpo.shape, lambda i: (0, 0), pipeline_mode=pl.Buffered(1)),
        pl.BlockSpec((rows, bonds * PAD), lambda i: (0, chunk), pipeline_mode=pl.Buffered(1)),
    ]
    if total is not None:
        operands.append(total)
        specs.append(pl.BlockSpec(block, late))
    aliases = {4: 0} if total is not None and dtype == jnp.float32 else {}
    size = 2 * (theta.size + left.size + rows * bonds * PAD) + 8 * rows * pairs * lanes
    return pl.pallas_call(
        functools.partial(forward_kernel, tiles, total is not None),
        grid=(tiles + pairs // 2,),
        out_shape=jax.ShapeDtypeStruct((parts, pairs, rows // parts, lanes), dtype),
        in_specs=specs,
        out_specs=pl.BlockSpec(block, late),
        scratch_shapes=[
            pltpu.VMEM((step, depth), jnp.bfloat16),
            pltpu.VMEM((tile, channels, pairs, lanes), jnp.bfloat16),
            pltpu.VMEM((pairs, bonds, PAD, lanes), jnp.bfloat16),
        ],
        input_output_aliases=aliases,
        compiler_params=params(),
        cost_estimate=cost(flops, size),
    )(*operands)


def exchange_kernel(pieces, term, full, near, mine, far, sent, got):
    col, chan = lax.axis_index("col"), lax.axis_index("chan")
    chans, count, rows, lanes = mine.shape
    group = count // pieces
    core, chip = {"col": 1 - col}, {"chan": 1 - chan}
    barrier = pltpu.get_barrier_semaphore()
    for peer in (core, chip):
        pl.semaphore_signal(barrier, inc=1, device_id=peer, device_id_type=pl.DeviceIdType.MESH)
    pl.semaphore_wait(barrier, 2)

    def copy(kind, j, source, target, peer):
        return pltpu.make_async_remote_copy(
            src_ref=source,
            dst_ref=target,
            send_sem=sent.at[kind, j],
            recv_sem=got.at[kind, j],
            device_id=peer,
            device_id_type=pl.DeviceIdType.MESH,
        )

    spans = [pl.ds(j * group, group) for j in range(pieces)]
    firsts = [
        copy(0, j, term.at[1 - col, :, spans[j]], near.at[:, spans[j]], core) for j in range(pieces)
    ]
    seconds = [copy(1, j, mine.at[:, spans[j]], far.at[:, spans[j]], chip) for j in range(pieces)]
    block = pl.ds(col * chans, chans)
    thirds = [
        copy(2, j, full.at[block, spans[j]], full.at[block, spans[j]], core) for j in range(pieces)
    ]
    for item in firsts:
        item.start()
    for j in range(pieces):
        firsts[j].wait_recv()

        def first(x, carry):
            for q in range(chans):
                value = term[col, q, x].astype(jnp.float32) + near[q, x].astype(jnp.float32)
                mine[q, x] = value.astype(jnp.bfloat16)
            return carry

        lax.fori_loop(j * group, (j + 1) * group, first, 0)
        seconds[j].start()
    for j in range(pieces):
        seconds[j].wait_recv()

        def second(x, carry):
            for q in range(chans):
                value = mine[q, x].astype(jnp.float32) + far[q, x].astype(jnp.float32)
                full[col * chans + q, x] = value.astype(jnp.bfloat16)
            return carry

        lax.fori_loop(j * group, (j + 1) * group, second, 0)
        thirds[j].start()
    for j in range(pieces):
        thirds[j].wait_recv()
    for item in firsts + seconds + thirds:
        item.wait_send()


def exchange(term):
    cols, chans, count, rows, lanes = term.shape
    pieces = 8
    half = pltpu.VMEM((chans, count, rows, lanes), jnp.bfloat16)
    return pl.pallas_call(
        functools.partial(exchange_kernel, pieces),
        out_shape=jax.ShapeDtypeStruct((cols * chans, count, rows, lanes), jnp.bfloat16),
        in_specs=[pl.BlockSpec(memory_space=pltpu.VMEM)],
        out_specs=pl.BlockSpec(memory_space=pltpu.VMEM),
        scratch_shapes=[half, half, half]
        + [pltpu.SemaphoreType.DMA((3, pieces)), pltpu.SemaphoreType.DMA((3, pieces))],
        compiler_params=pltpu.CompilerParams(
            collective_id=0, has_side_effects=True, vmem_limit_bytes=LIMIT
        ),
        cost_estimate=cost(0, 4 * term.size),
    )(term)


def backward_kernel(groups, right_ref, *refs):
    res_refs = refs[:groups]
    mpo_ref, left_ref, out_ref, held, lhs = refs[groups:]
    tile, _, _, lanes = held.shape
    channels = lhs.shape[1] // lanes
    pairs = lhs.shape[0] // tile
    width = out_ref.shape[2]
    begin = 0
    for res_ref in res_refs:
        parts, count, rows, _ = res_ref.shape

        def five(x, carry, res_ref=res_ref, begin=begin, depth=parts * rows):
            first = res_ref[:, 2 * x].reshape(depth, lanes)
            second = res_ref[:, 2 * x + 1].reshape(depth, lanes)
            part = pair_dot(right_ref[...], first, second)
            held[:, begin + 2 * x] = part[:, :lanes].reshape(tile, PAD, lanes)
            held[:, begin + 2 * x + 1] = part[:, lanes:].reshape(tile, PAD, lanes)
            return carry

        lax.fori_loop(0, count // 2, five, 0, unroll=2)
        begin += count

    def six(b, carry):
        first = held[2 * b].reshape(begin * PAD, lanes)
        second = held[2 * b + 1].reshape(begin * PAD, lanes)
        part = pair_dot(mpo_ref[...], first, second)
        for j in range(2):
            where = pl.ds(pl.multiple_of((2 * b + j) * pairs, pairs), pairs)
            half = part[:, j * lanes : (j + 1) * lanes]
            for w in range(channels):
                lhs[where, w * lanes : (w + 1) * lanes] = half[w * pairs : (w + 1) * pairs]
        return carry

    lax.fori_loop(0, tile // 2, six, 0, unroll=4)

    for r in range(0, out_ref.shape[0], 2):
        part = dot(lhs[...], left_ref[:, r * width : (r + 2) * width]).astype(jnp.bfloat16)
        out_ref[r] = part[:, :width]
        out_ref[r + 1] = part[:, width:]


def backward(right, residuals, mpo, left, chunk, bonds, pairs, blocks, tile):
    depth, lanes = residuals[0].shape[0] * residuals[0].shape[2], residuals[0].shape[3]
    channels = left.shape[0] // lanes
    width = left.shape[1] // blocks
    steps = bonds // tile
    counts = sum(res.shape[1] for res in residuals)
    flops = 2 * bonds * (PAD * depth * counts * lanes + mpo.size * lanes + pairs * left.size)
    size = 2 * (depth * counts * lanes + left.size + bonds * PAD * depth + bonds * pairs * left.shape[1])
    whole = [
        pl.BlockSpec(res.shape, lambda i: (0, 0, 0, 0), pipeline_mode=pl.Buffered(1))
        for res in residuals
    ]
    return pl.pallas_call(
        functools.partial(backward_kernel, len(residuals)),
        grid=(steps,),
        out_shape=jax.ShapeDtypeStruct((blocks, bonds * pairs, width), jnp.bfloat16),
        in_specs=[pl.BlockSpec((tile * PAD, depth), lambda i: (chunk * steps + i, 0))]
        + whole
        + [
            pl.BlockSpec(mpo.shape, lambda i: (0, 0), pipeline_mode=pl.Buffered(1)),
            pl.BlockSpec(left.shape, lambda i: (0, 0), pipeline_mode=pl.Buffered(1)),
        ],
        out_specs=pl.BlockSpec((blocks, tile * pairs, width), lambda i: (0, i, 0)),
        scratch_shapes=[
            pltpu.VMEM((tile, counts, PAD, lanes), jnp.bfloat16),
            pltpu.VMEM((tile * pairs, channels * lanes), jnp.bfloat16),
        ],
        compiler_params=params(),
        cost_estimate=cost(flops, size),
    )(right, *residuals, mpo, left)


def mpo_product(mpo_left, mpo_right):
    paired = jnp.einsum("wuxs,uvyt->wstxyv", mpo_left, mpo_right, precision=lax.Precision.HIGHEST)
    channels, phys = mpo_left.shape[0], mpo_left.shape[2]
    return paired.reshape(channels * phys * phys, phys * phys * channels).astype(jnp.bfloat16)


def tiled_shards(theta, left_env, right_env, mpo_left, mpo_right):
    lanes, channels, depth = left_env.shape
    pairs, bonds = theta.shape[1:]
    width = theta.shape[0]
    blocks = lax.axis_size("row")
    cols, chans = lax.axis_size("col"), lax.axis_size("chan")
    parts = cols * chans
    chunks = 4
    size = bonds // chunks
    tile = min(32, size)
    rows = right_env.shape[0]

    turned = jnp.transpose(theta, (2, 1, 0)).reshape(chunks, size * pairs, width)
    gathered = [lax.all_gather(turned[c], "row", axis=0) for c in range(chunks)]

    mpo = mpo_product(mpo_left, mpo_right).reshape(channels * pairs, pairs, channels)
    mpo = jnp.pad(mpo, ((0, 0), (0, 0), (0, PAD - channels)))
    mpo_back = mpo.reshape(channels * pairs, pairs * PAD)
    mpo_front = mpo_back.T
    left_front = left_env.reshape(lanes, channels // 2, 2, depth)
    left_front = jnp.transpose(left_front, (1, 3, 2, 0)).reshape(channels // 2, depth, 2 * lanes)
    left_back = jnp.transpose(left_env, (1, 0, 2)).reshape(channels * lanes, depth)
    right_back = jnp.transpose(right_env, (2, 1, 0))
    right_back = jnp.pad(right_back, ((0, 0), (0, PAD - channels), (0, 0)))
    right_back = right_back.reshape(bonds * PAD, rows)
    right_front = right_back.T

    total = None
    for c in range(chunks):
        dtype = jnp.bfloat16 if c == chunks - 1 else jnp.float32
        total = forward(
            gathered[c], left_front, mpo_front, right_front, total, c, pairs, tile, parts, dtype
        )
    full = exchange(total.reshape(cols, chans, pairs, rows // parts, lanes))
    mine = lax.axis_index("col") * chans + lax.axis_index("chan")
    kept = lax.dynamic_index_in_dim(full, mine, 0, keepdims=False)
    residuals = [full]

    products = []
    for c in range(chunks):
        part = backward(
            right_back, residuals, mpo_back, left_back, c, size, pairs, blocks, tile
        )
        products.append(lax.psum_scatter(part, "row", scatter_dimension=0))
    product = jnp.concatenate(products, axis=0).reshape(bonds, pairs, width)
    residual = jnp.transpose(kept, (1, 2, 0))
    return residual.reshape(rows // parts, lanes * pairs), jnp.transpose(product, (2, 1, 0))


def plain_shards(theta, left_env, right_env, mpo_left, mpo_right):
    left_rows, channels = left_env.shape[:2]
    pairs, right_rows = theta.shape[1:]
    mpo_pair = mpo_product(mpo_left, mpo_right)
    einsum = functools.partial(jnp.einsum, preferred_element_type=jnp.float32)
    one = einsum("awk,ksb->awsb", left_env, lax.all_gather(theta, "row", axis=0, tiled=True))
    one = one.astype(jnp.bfloat16).reshape(left_rows, channels * pairs, right_rows)
    three = einsum("pq,apb->aqb", mpo_pair, one).astype(jnp.bfloat16)
    three = three.reshape(left_rows, pairs, channels, right_rows)
    term = einsum("kvb,asvb->kas", right_env, three).astype(jnp.bfloat16)
    term = term.reshape(right_env.shape[0], left_rows * pairs)
    residual = lax.psum_scatter(term, ("col", "chan"), scatter_dimension=0, tiled=True)
    full = lax.all_gather(residual, ("col", "chan"), axis=0, tiled=True)
    back = einsum("kp,kvb->pvb", full, right_env).astype(jnp.bfloat16)
    back = back.reshape(left_rows, pairs * channels, right_rows)
    back = einsum("pq,aqb->apb", mpo_pair, back).astype(jnp.bfloat16)
    back = back.reshape(left_rows, channels, pairs, right_rows)
    product = einsum("awk,awsb->ksb", left_env, back).astype(jnp.bfloat16)
    return residual, lax.psum_scatter(product, "row", scatter_dimension=0, tiled=True)


def shards(theta, left_env, right_env, mpo_left, mpo_right):
    wide = left_env.shape[0] % 128 == 0 and theta.shape[0] % 128 == 0
    wide = wide and theta.shape[2] % 128 == 0 and theta.shape[1] == PAD
    wide = wide and lax.axis_size("col") == 2 and lax.axis_size("chan") == 2
    wide = wide and left_env.shape[1] % 2 == 0 and lax.axis_size("row") % 2 == 0
    body = tiled_shards if wide and left_env.shape[1] <= PAD else plain_shards
    return body(theta, left_env, right_env, mpo_left, mpo_right)


def solution(mesh):
    in_specs = (
        P(("grp", "row"), None, ("col", "chan")),
        P(("grp", "row"), None, None),
        P("grp", None, ("col", "chan")),
        P(),
        P(),
    )
    out_specs = (P(("grp", "col", "chan"), "row"), P(("grp", "row"), None, ("col", "chan")))
    return jax.shard_map(shards, mesh=mesh, in_specs=in_specs, out_specs=out_specs, check_vma=False)
```

time: 712 us -> 562 us (0.79)
  waiting for transfers between devices: 325 us -> 118 us
  Pallas kernels: 273 us -> 329 us
    all_gather x4 -> x0, waiting for transfers between devices: 99.2 us -> none  [the longest x2 67.8 us: tiled_shards(): lax.all_gather(kept[h], 'chan', axis=0)]
    reduce_scatter x4 -> x0, waiting for transfers between devices: 76.9 us -> none  [the longest x2 66.8 us: tiled_shards(): term = lax.psum_scatter(term, 'chan', scatter_dimension=0)]
    pallas_call x9 -> x5, Pallas kernels: 161 us -> 223 us  [the longest x4 119 us: forward(): pl.pallas_call(functools.partial(forward_kernel, tiles, total is not None...]
    all_gather x4, waiting for transfers between devices: 54.1 us -> 27.7 us  [tiled_shards(): gathered = [lax.all_gather(turned[c], 'row', axis=0) for c in range(chunks)]]
    reshape x2, local copies, waits for them, and re-layouts: 15.7 us -> 27 us  [the longest x1 16.1 us: tiled_shards(): left_front = left_env.reshape(lanes, channels // 2, 2, depth)]
    unnamed x12 -> x9, local copies, waits for them, and re-layouts: 24.1 us -> 16.7 us
  transfers between devices with their start and end apart: 16 -> 8, of which waited for: 12 -> 4; matrix products, arithmetic and copies ran while one was open for 10% -> 14% of each run, Pallas kernels for 31% -> 31%
where the time goes in v2:
time: 562 us; the launch traced here: 555 us
  Pallas kernels  329 us (59%)
  waiting for transfers between devices  118 us (21%)
  local copies, waits for them, and re-layouts  88.7 us (16%)
  between operations  14.5 us (3%)
    pallas_call x4, Pallas kernels, forward(): pl.pallas_call(functools.partial(forward_kernel, tiles, total is not None...  119 us
    pallas_call x4, Pallas kernels, backward(): pl.pallas_call(functools.partial(backward_kernel, len(residuals)), grid=(...  107 us
    pallas_call x1, Pallas kernels, exchange(): pl.pallas_call(functools.partial(exchange_kernel, pieces), out_shape=jax....  103 us
    reduce_scatter x4, waiting for transfers between devices, tiled_shards(): products.append(lax.psum_scatter(part, 'row', scatter_dimension=0))  89.8 us
    all_gather x4, waiting for transfers between devices, tiled_shards(): gathered = [lax.all_gather(turned[c], 'row', axis=0) for c in range(chunks)]  27.7 us
    unnamed x9, local copies, waits for them, and re-layouts  16.7 us
    reshape x1, local copies, waits for them, and re-layouts, tiled_shards(): left_front = left_env.reshape(lanes, channels // 2, 2, depth)  16.1 us
    slice x5, local copies, waits for them, and re-layouts, tiled_shards(): gathered = [lax.all_gather(turned[c], 'row', axis=0) for c in range(chunks)]  14.1 us
  transfers between devices with their start and end apart: 8, of which 4 were waited for; matrix products, arithmetic and copies ran while one was open for 14% of the time, Pallas kernels for 31%

profile of v2, /device:TPU:0, one launch (start us, length us, event | category | flops | bytes accessed | tf_op | source)
XLA Modules:
  0.0 554.6 jit_solution(7081184550821008660)
XLA Ops:
  7.2 4.2 fusion.3
  11.4 3.5 copy.56
  14.9 2.2 copy.55
  17.2 2.2 copy.54
  19.4 2.2 copy.47
  21.6 0.6 reduce-scatter.5.cloned.1.call-start
  22.1 11.9 %copy.75 = bf16[256,12,1024]{2,1,0:T(8,128)(2,1)} copy(bf16[256,12,1024]{0,2,1:T(8,128)(2,1)} %bitcast.50) | data formatting | bytes 12582912
  34.1 8.9 %pad.9.clone = bf16[256,16,1024]{2,1,0:T(8,128)(2,1)} pad(bf16[256,12,1024]{2,1,0:T(8,128)(2,1)} %copy.75, bf16[]{:T(256)} %constant.12.clone.1), padding=0_0x0_4x0_0 | pad | bytes 14680066 | tf_op jit(solution)/shard_map/jit(_pad)/pad | solution.py:294
  43.0 11.3 %copy.60.right_ref = bf16[1024,4096]{1,0:T(8,128)(2,1)} copy(bf16[1024,4096]{0,1:T(8,128)(2,1)} %bitcast.40) | data formatting | bytes 16777216 | tf_op jit(solution)/shard_map/transpose | solution.py:296
  54.3 1.9 fusion
  56.1 2.3 copy.51
  58.4 0.7 copy.74
  59.2 16.1 %copy.48 = bf16[256,6,2,1024]{0,2,3,1:T(2,128)(2,1)} copy(bf16[256,6,2,1024]{3,0,2,1:T(8,128)(2,1)} %bitcast.51) | data formatting | bytes 12582912 | tf_op jit(solution)/shard_map/reshape | solution.py:290
  75.3 10.8 %reshape.38.left_ref = bf16[6,1024,512]{2,1,0:T(8,128)(2,1)} reshape(bf16[6,1024,2,256]{3,2,1,0:T(2,128)(2,1)} %bitcast.45) | data formatting | bytes 12582912 | tf_op jit(solution)/shard_map/reshape | solution.py:291
  86.3 26.7 %shard_map.68.refs_0_ = f32[4,16,256,256]{3,2,1,0:T(8,128)} custom-call(bf16[4,1024,256]{2,1,0:T(8,128)(2,1)} %all-gather.11.cloned.1.call-done.theta_ref, bf16[6,1024,512]{2,1,0:T(8,128)(2,1)} %reshape.38.left_ref, bf16[256,192]{1,0:T(8,128)(2,1)S(1)} %bitcast.36, bf16[1024,4096]{1,0:T(8,128)(2,1)} %copy.60.right_ref), custom_call_target="tpu_custom_call" | custom-call | flops 16642998272 | bytes 44040192 | tf_op jit(solution)/shard_map/pallas_call | solution.py:98
  113.0 31.3 %shard_map.69.refs_0_ = f32[4,16,256,256]{3,2,1,0:T(8,128)} custom-call(bf16[4,1024,256]{2,1,0:T(8,128)(2,1)} %all-gather.9.cloned.1.call-done.theta_ref, bf16[6,1024,512]{2,1,0:T(8,128)(2,1)} %reshape.38.left_ref, bf16[256,192]{1,0:T(8,128)(2,1)S(1)} %bitcast.37, bf16[1024,4096]{1,0:T(8,128)(2,1)} %copy.60.right_ref, ...), custom_call_target="tpu_custom_call", output_to_operand_aliasing={{}: (4, {})} | custom-call | flops 16642998272 | bytes 44040192 | tf_op jit(solution)/shard_map/pallas_call | solution.py:98
  144.4 12.4 %all-gather.7.cloned.1.call-done.theta_ref = bf16[4,1024,256]{2,1,0:T(8,128)(2,1)} async-done(((bf16[1,1024,256]{2,1,0:T(8,128)(2,1)}), bf16[4,1024,256]{2,1,0:T(8,128)(2,1)}) %all-gather.7.cloned.1.call-update) | async-done | bytes 2097168 | tf_op jit(solution)/shard_map/all_gather | solution.py:284
  156.8 31.4 %shard_map.70.refs_0_ = f32[4,16,256,256]{3,2,1,0:T(8,128)} custom-call(bf16[4,1024,256]{2,1,0:T(8,128)(2,1)} %all-gather.7.cloned.1.call-done.theta_ref, bf16[6,1024,512]{2,1,0:T(8,128)(2,1)} %reshape.38.left_ref, bf16[256,192]{1,0:T(8,128)(2,1)S(1)} %bitcast.38, bf16[1024,4096]{1,0:T(8,128)(2,1)} %copy.60.right_ref, ...), custom_call_target="tpu_custom_call", output_to_operand_aliasing={{}: (4, {})} | custom-call | flops 16642998272 | bytes 44040192 | tf_op jit(solution)/shard_map/pallas_call | solution.py:98
  188.2 15.3 %all-gather.5.cloned.1.call-done.theta_ref = bf16[4,1024,256]{2,1,0:T(8,128)(2,1)} async-done(((bf16[1,1024,256]{2,1,0:T(8,128)(2,1)}), bf16[4,1024,256]{2,1,0:T(8,128)(2,1)}) %all-gather.5.cloned.1.call-update) | async-done | bytes 2097168 | tf_op jit(solution)/shard_map/all_gather | solution.py:284
  203.5 29.6 %shard_map.71 = bf16[4,16,256,256]{3,2,1,0:T(8,128)(2,1)} custom-call(bf16[4,1024,256]{2,1,0:T(8,128)(2,1)} %all-gather.5.cloned.1.call-done.theta_ref, bf16[6,1024,512]{2,1,0:T(8,128)(2,1)} %reshape.38.left_ref, bf16[256,192]{1,0:T(8,128)(2,1)S(1)} %bitcast.39, bf16[1024,4096]{1,0:T(8,128)(2,1)} %copy.60.right_ref, f32[4,16,256,256]{3,2,1,0:T(8,128)} %shard_map.70.refs_0_), custom_call_target="tpu_custom_call" | custom-call | flops 16642998272 | bytes 44040192 | tf_op jit(solution)/shard_map/pallas_call | solution.py:98
  233.0 103.5 %shard_map.72.refs_0_ = bf16[4,16,256,256]{3,2,1,0:T(8,128)(2,1)} custom-call(bf16[2,2,16,256,256]{4,3,2,1,0:T(8,128)(2,1)} %bitcast.46), custom_call_target="tpu_custom_call" | custom-call | bytes 16777216 | tf_op jit(solution)/shard_map/pallas_call | solution.py:178
  336.5 26.5 %shard_map.73 = bf16[4,1024,256]{2,1,0:T(8,128)(2,1)} custom-call(bf16[4096,1024]{1,0:T(8,128)(2,1)} %bitcast.41, bf16[4,16,256,256]{3,2,1,0:T(8,128)(2,1)} %shard_map.72.refs_0_, bf16[192,256]{1,0:T(8,128)(2,1)S(1)} %copy.62.refs_1_, bf16[3072,1024]{1,0:T(8,128)(2,1)} %bitcast.52), custom_call_target="tpu_custom_call" | custom-call | flops 16642998272 | bytes 18874368 | tf_op jit(solution)/shard_map/pallas_call | solution.py:245
  363.1 27.1 %shard_map.74 = bf16[4,1024,256]{2,1,0:T(8,128)(2,1)} custom-call(bf16[4096,1024]{1,0:T(8,128)(2,1)} %bitcast.42, bf16[4,16,256,256]{3,2,1,0:T(8,128)(2,1)} %shard_map.72.refs_0_, bf16[192,256]{1,0:T(8,128)(2,1)S(1)} %copy.62.refs_1_, bf16[3072,1024]{1,0:T(8,128)(2,1)} %bitcast.53), custom_call_target="tpu_custom_call" | custom-call | flops 16642998272 | bytes 18874368 | tf_op jit(solution)/shard_map/pallas_call | solution.py:245
  390.2 26.5 %shard_map.75 = bf16[4,1024,256]{2,1,0:T(8,128)(2,1)} custom-call(bf16[4096,1024]{1,0:T(8,128)(2,1)} %bitcast.43, bf16[4,16,256,256]{3,2,1,0:T(8,128)(2,1)} %shard_map.72.refs_0_, bf16[192,256]{1,0:T(8,128)(2,1)S(1)} %copy.62.refs_1_, bf16[3072,1024]{1,0:T(8,128)(2,1)} %bitcast.54), custom_call_target="tpu_custom_call" | custom-call | flops 16642998272 | bytes 18874368 | tf_op jit(solution)/shard_map/pallas_call | solution.py:245
  416.8 26.8 %shard_map.76 = bf16[4,1024,256]{2,1,0:T(8,128)(2,1)} custom-call(bf16[4096,1024]{1,0:T(8,128)(2,1)} %bitcast.44, bf16[4,16,256,256]{3,2,1,0:T(8,128)(2,1)} %shard_map.72.refs_0_, bf16[192,256]{1,0:T(8,128)(2,1)S(1)} %copy.62.refs_1_, bf16[3072,1024]{1,0:T(8,128)(2,1)} %bitcast.55), custom_call_target="tpu_custom_call" | custom-call | flops 16642998272 | bytes 18874368 | tf_op jit(solution)/shard_map/pallas_call | solution.py:245
  443.7 1.7 dynamic-slice_bitcast_fusion
  445.4 3.1 copy.61
  448.5 4.1 copy.67
  452.5 44.2 %reduce-scatter.9.cloned.1.call-done = bf16[1,1024,256]{2,1,0:T(8,128)(2,1)} async-done(((bf16[4,1024,256]{2,1,0:T(8,128)(2,1)}), bf16[1,1024,256]{2,1,0:T(8,128)(2,1)}) %reduce-scatter.9.cloned.1.call-update) | async-done | bytes 524304 | tf_op jit(solution)/shard_map/reduce_scatter | solution.py:314
  496.8 45.6 %reduce-scatter.11.cloned.1.call-done = bf16[1,1024,256]{2,1,0:T(8,128)(2,1)} async-done(((bf16[4,1024,256]{2,1,0:T(8,128)(2,1)}), bf16[1,1024,256]{2,1,0:T(8,128)(2,1)}) %reduce-scatter.11.cloned.1.call-update) | async-done | bytes 524304 | tf_op jit(solution)/shard_map/reduce_scatter | solution.py:314
  542.4 1.7 pad_maximum_fusion
  544.1 3.5 copy.66
  (27 shorter events, 0.6 us)
Async XLA Ops:
  7.2 47.1 %copy-start = (f32[12,12,4,4]{1,3,2,0:T(4,128)S(1)}, f32[12,12,4,4]{1,3,2,0:T(4,128)}, u32[]{:S(2)}) copy-start(f32[12,12,4,4]{1,3,2,0:T(4,128)} %param.8) | copy-start | bytes 27652
  7.2 79.1 %all-gather.11.cloned.1.call-start = ((), (), s32[]{:S(2)}) async-start(), calls=%async_computation.7 | async-start | bytes 2621440 | tf_op jit(solution)/shard_map/all_gather | solution.py:284
  14.9 98.2 %all-gather.9.cloned.1.call-start = ((), (), s32[]{:S(2)}) async-start(), calls=%async_computation.6 | async-start | bytes 2621440 | tf_op jit(solution)/shard_map/all_gather | solution.py:284
  17.1 139.7 %all-gather.7.cloned.1.call-start = ((), (), s32[]{:S(2)}) async-start(), calls=%async_computation.5 | async-start | bytes 2621440 | tf_op jit(solution)/shard_map/all_gather | solution.py:284
  19.3 184.1 %all-gather.5.cloned.1.call-start = ((), (), s32[]{:S(2)}) async-start(), calls=%async_computation.4 | async-start | bytes 2621440 | tf_op jit(solution)/shard_map/all_gather | solution.py:284
  21.6 431.0 %reduce-scatter.5.cloned.1.call-start = ((), (), s32[]{:S(2)}) async-start(), calls=%async_computation.8 | async-start | bytes 2621440 | tf_op jit(solution)/shard_map/reduce_scatter | solution.py:314
  43.0 11.3 %copy-start.2 = (f32[12,12,4,4]{1,3,2,0:T(4,128)S(1)}, f32[12,12,4,4]{1,3,2,0:T(4,128)}, u32[]{:S(2)}) copy-start(f32[12,12,4,4]{1,3,2,0:T(4,128)} %param.9) | copy-start | bytes 27652
  363.0 89.5 %reduce-scatter.7.cloned.1.call-start = ((), (), s32[]{:S(2)}) async-start(), calls=%async_computation.9 | async-start | bytes 2621440 | tf_op jit(solution)/shard_map/reduce_scatter | solution.py:314
  390.2 106.6 %reduce-scatter.9.cloned.1.call-start = ((), (), s32[]{:S(2)}) async-start(), calls=%async_computation.10 | async-start | bytes 2621440 | tf_op jit(solution)/shard_map/reduce_scatter | solution.py:314
  416.8 125.6 %reduce-scatter.11.cloned.1.call-start = ((), (), s32[]{:S(2)}) async-start(), calls=%async_computation.11 | async-start | bytes 2621440 | tf_op jit(solution)/shard_map/reduce_scatter | solution.py:314
  544.0 3.5 copy-start.1
Sparse Core Ops, SparseCore 0:
  15.0 48.6 all-gather.10
  65.2 44.6 all-gather.8
  112.1 44.6 all-gather.6
  158.8 44.6 all-gather.4
  363.1 42.5 reduce-scatter.4
  408.0 43.2 reduce-scatter.6
  453.5 43.1 reduce-scatter.8
  499.2 43.1 reduce-scatter.10
